TPU v7x, 32 devices: a whole 2x2x4 slice. The times are simulated.
32 devices in a mesh: ctx: 8 (over y, x, core), chan: 4 (over z).
Axes of the slice: x: 2, y: 2, z: 4, core: 2. Of those that a mesh axis runs over, the one named last changes fastest.
Arguments:
- features: bfloat16 [3, 8192, 4096], P(None, 'chan', 'ctx'), may hold values from -6 to 6
- short_filter: float32 [3, 3, 8192], P(None, None, 'chan'), may hold values from -3.5 to 3.5
- lengths: int32 [8], P('ctx'), may hold values from 64 to 512, as said below
- offsets: int32 [8], P('ctx'), may hold values from 0 to 8128, as said below
- decay_rates: float32 [16, 1024], P(None, 'chan'), may hold values from 0 to 1, as said below
- residues: float32 [16, 1024], P(None, 'chan'), may hold values from -1 to 1
- skip_weight: float32 [8192], P('chan'), may hold values from -1 to 1
- out_weight: bfloat16 [8192, 4096], P('chan'), may hold values from -0.09375 to 0.09375
Outputs:
- projected: bfloat16 [4096, 4096], P('chan', 'ctx')
Inputs may be any that keep to these rules, and one draw needn't show every extreme that they name: `lengths`: used slots of each shard, counted from slot 0; some shard uses all 512 slots and some only 64. offsets[i] + lengths[i] <= offsets[i + 1]; the first offset is 0. `decay_rates`: positive rates.
All inputs are finite; a program needn't handle non-finite values.
Results may differ from a plain program's by a relative error of at most 0.018.
Values may be sent and summed in bfloat16 or wider, within the bound.
No kernel may reach another device: no remote copies, remote signals or barrier semaphores. Data moves between devices by JAX's collectives and lax.ppermute only.
A program may use at most 192 MiB of HBM per device.

v0:
```python
import jax
import jax.numpy as jnp
from jax import lax
from jax.sharding import PartitionSpec as P

highest = lax.Precision.HIGHEST


def passed_along(array, axis, by):
    length = lax.axis_size(axis)
    pairs = [(i, i + by) for i in range(length) if 0 <= i + by < length]
    return lax.ppermute(array, axis, pairs)


def shortened(array):
    return jax.tree.map(lambda a: a.astype(jnp.bfloat16) if a.dtype == jnp.float32 else a, array)


def block_pass(blocks, firsts, counts, decay_rows, residue):
    groups, per_group, block_count, block_width = blocks.shape
    mode_count = decay_rows.shape[0]
    rate_g = decay_rows.T
    residue_g = residue.T
    lag_index = jnp.arange(block_width)
    lag_float = lag_index.astype(jnp.float32)
    to_end = jnp.exp(-rate_g[:, None, :] * (block_width - 1.0 - lag_float)[None, :, None])
    raw_sums = lax.dot_general(
        blocks.reshape(groups, per_group * block_count, block_width),
        to_end,
        (((2,), (1,)), ((0,), (0,))),
        precision=highest,
    )
    lift = jnp.exp(rate_g[:, None, :] * (block_width - counts.astype(jnp.float32))[None, :, None])
    summary = raw_sums.reshape(groups, per_group, block_count, mode_count) * lift[:, None, :, :]
    difference = (lag_index[:, None] - lag_index[None, :]).astype(jnp.float32)
    distance = jnp.maximum(difference, 0.0)
    toeplitz = jnp.zeros((groups, block_width, block_width), jnp.float32)
    for mode_index in range(mode_count):
        toeplitz = toeplitz + residue_g[:, mode_index, None, None] * jnp.exp(
            -rate_g[:, mode_index, None, None] * distance[None]
        )
    toeplitz = jnp.where((difference >= 0.0)[None], toeplitz, 0.0)
    inner_part = lax.dot_general(blocks, toeplitz, (((3,), (2,)), ((0,), (0,))), precision=highest)
    lasts = firsts + counts.astype(jnp.float32) - 1.0
    gap_matrix = jnp.maximum(firsts[None, :] - lasts[:, None], 0.0)
    earlier_mask = lag_index[:block_count, None] < lag_index[None, :block_count]
    mixing = jnp.where(
        earlier_mask[None, None], jnp.exp(-rate_g[:, :, None, None] * gap_matrix[None, None]), 0.0
    )
    entering = jnp.einsum("gkcm,gmcb->gkbm", summary, mixing, precision=highest)
    return (inner_part, summary, entering, lasts)


def outer_pass(entering, decay_rows, residue, block_width):
    groups, per_group, block_count, mode_count = entering.shape
    rate_g = decay_rows.T
    lag_float = jnp.arange(block_width, dtype=jnp.float32)
    spread_values = residue.T[:, :, None] * jnp.exp(-rate_g[:, :, None] * lag_float[None, None, :])
    outer_part = lax.dot_general(
        entering.reshape(groups, per_group * block_count, mode_count),
        spread_values,
        (((2,), (1,)), ((0,), (0,))),
        precision=highest,
    )
    return outer_part.reshape(groups, per_group, block_count, block_width)


def shards(
    features, short_filter, lengths, offsets, decay_rates, residues, skip_weight, out_weight
):
    kernel_taps = short_filter.shape[1]
    channels = features.shape[1]
    slot_count = features.shape[2]
    groups = decay_rates.shape[1]
    per_group = channels // groups
    block_width = min(128, slot_count)
    length = lengths[0]
    tail_rows = lax.dynamic_slice_in_dim(
        features, length - (kernel_taps - 1), kernel_taps - 1, axis=2
    )
    previous = passed_along(tail_rows, "ctx", 1)
    extended = jnp.concatenate([previous, features], axis=2)
    short_conv = jnp.zeros((3, channels, slot_count), jnp.float32)
    for tap_index in range(kernel_taps):
        window_rows = lax.slice_in_dim(
            extended, kernel_taps - 1 - tap_index, kernel_taps - 1 - tap_index + slot_count, axis=2
        )
        short_conv = short_conv + short_filter[:, tap_index, :, None] * window_rows.astype(
            jnp.float32
        )
    usable = jnp.arange(slot_count) < length
    product = jnp.where(usable, short_conv[1] * short_conv[2], 0.0)
    all_lengths, all_offsets = (
        lax.all_gather(lengths, "ctx", axis=0, tiled=True),
        lax.all_gather(offsets, "ctx", axis=0, tiled=True),
    )
    ctx_count = lax.axis_size("ctx")
    rank_self = lax.axis_index("ctx")
    shared = groups // ctx_count
    decay_mine = lax.dynamic_slice_in_dim(decay_rates, rank_self * shared, shared, 1)
    residue_mine = lax.dynamic_slice_in_dim(residues, rank_self * shared, shared, 1)
    per_shard = slot_count // block_width
    within = jnp.tile(jnp.arange(per_shard) * block_width, ctx_count)
    firsts_all = jnp.repeat(all_offsets, per_shard).astype(jnp.float32) + within.astype(jnp.float32)
    counts_all = jnp.clip(jnp.repeat(all_lengths, per_shard) - within, 0, block_width)
    received = lax.all_to_all(
        product.reshape(groups, per_group, slot_count).astype(jnp.bfloat16),
        "ctx",
        split_axis=0,
        concat_axis=2,
        tiled=True,
    ).astype(jnp.float32)
    item_count = received.shape[1]
    blocks = received.reshape(shared, item_count, ctx_count * per_shard, block_width)
    inner_part, summary, entering, lasts = block_pass(
        blocks, firsts_all, counts_all, decay_mine, residue_mine
    )
    outer_part = outer_pass(entering, decay_mine, residue_mine, block_width)
    result = (inner_part + outer_part).reshape(shared, item_count, ctx_count * slot_count)
    long_conv = lax.all_to_all(
        shortened(result), "ctx", split_axis=2, concat_axis=0, tiled=True
    ).astype(result.dtype)
    long_conv = long_conv.reshape(channels, slot_count)
    mixed_rows = jnp.where(
        usable, short_conv[0] * (long_conv + skip_weight[:, None] * product), 0.0
    ).astype(jnp.bfloat16)
    return lax.psum_scatter(
        lax.dot_general(
            out_weight, mixed_rows, (((0,), (0,)), ((), ())), preferred_element_type=jnp.float32
        ).astype(jnp.bfloat16),
        "chan",
        scatter_dimension=0,
        tiled=True,
    )


def solution(mesh):
    placed = (
        P(None, "chan", "ctx"),
        P(None, None, "chan"),
        P("ctx"),
        P("ctx"),
        P(None, "chan"),
        P(None, "chan"),
        P("chan"),
        P("chan", None),
    )
    return jax.shard_map(
        shards, mesh=mesh, in_specs=placed, out_specs=P("chan", "ctx"), check_vma=False
    )
```

profile of v0, /device:TPU:0, one launch (start us, length us, event | category | flops | bytes accessed | tf_op | source)
XLA Modules:
  0.0 309.9 jit_solution(4460304330251844339)
XLA Ops:
  6.5 0.0 copy-start
  7.2 0.0 copy-start.8
  7.2 0.0 copy-start.5
  7.2 2.5 constant_dynamic-slice_fusion
  9.7 0.9 copy.54
  10.6 2.4 collective-permute-start
  13.6 0.0 copy-done.8
  13.6 0.6 dynamic-slice
  14.3 0.7 dynamic-update-slice.1
  15.0 0.7 dynamic-update-slice
  15.8 9.1 %all-reduce.2 = (s32[8]{0:T(128)S(1)}, s32[8]{0:T(128)S(1)}) all-reduce(s32[8]{0:T(128)S(1)} %dynamic-update-slice, s32[8]{0:T(128)S(1)} %dynamic-update-slice.1), channel_id=1, replica_groups=mesh['ctx'=8,'chan'=4] {'ctx'}, use_global_device_ids=true, to_apply=%add | all-reduce | flops 16 | bytes 128
  24.8 0.0 copy-done.5
  24.8 0.1 fusion.155
  24.9 0.1 clamp_convert_fusion
  24.9 0.1 broadcast_add_fusion
  25.1 0.0 collective-permute-done
  25.1 0.9 copy.38
  26.0 12.5 %multiply_add_fusion = f32[3,2048,512]{2,1,0:T(8,128)S(1)} fusion(bf16[3,2048,512]{2,1,0:T(8,128)(2,1)} %param.8, bf16[3,2048,2]{2,1,0:T(8,128)(2,1)S(1)} %copy.38, f32[3,2048]{1,0:T(4,128)S(1)} %get-tuple-element.46, f32[3,2048]{1,0:T(4,128)S(1)} %get-tuple-element.47, f32[3,2048]{1,0:T(4,128)S(1)} %bitcast.143), kind=kLoop, calls=%fused_computation.1 | loop fusion | flops 44040192 | bytes 18972672 | tf_op jit(solution)/shard_map/add | solution.py:88
  38.5 0.0 copy-start.2
  38.5 4.5 %copy-done.2 = f32[3,2048,512]{2,1,0:T(8,128)} copy-done((f32[3,2048,512]{2,1,0:T(8,128)}, f32[3,2048,512]{2,1,0:T(8,128)S(1)}, u32[]{:S(2)}) %copy-start.2) | copy-done | bytes 12582936
  43.1 2.5 fusion.11
  45.5 0.0 copy-start.7
  45.5 3.7 %all-to-all-start = ((bf16[256,8,512]{2,1,0:T(8,128)(2,1)}), bf16[256,8,512]{2,1,0:T(8,128)(2,1)S(1)}, u32[]{:S(2)}, u32[]{:S(2)}) async-start(bf16[256,8,512]{2,1,0:T(8,128)(2,1)} %fusion.11), calls=%async_computation | async-start | bytes 4194304 | tf_op jit(solution)/shard_map/all_to_all | solution.py:106
  49.3 0.0 reduce-scatter.2.cloned.1.call-start
  49.3 0.0 copy-done
  49.3 0.1 dynamic-slice_bitcast_fusion.1
  49.4 0.1 convert_element_type.139
  49.5 0.1 add.115
  49.6 0.1 copy.44
  49.7 0.0 copy-done.7
  49.7 0.1 fusion.154
  49.7 0.1 copy.40
  49.8 0.1 copy.43
  50.0 0.1 broadcast_compare_fusion
  50.1 0.1 subtract_maximum_fusion
  50.2 0.1 multiply_exponential_fusion
  50.3 25.6 %all-to-all-done = bf16[256,8,512]{2,1,0:T(8,128)(2,1)S(1)} async-done(((bf16[256,8,512]{2,1,0:T(8,128)(2,1)}), bf16[256,8,512]{2,1,0:T(8,128)(2,1)S(1)}, u32[]{:S(2)}, u32[]{:S(2)}) %all-to-all-start) | async-done | bytes 2097184 | tf_op jit(solution)/shard_map/all_to_all | solution.py:106
  75.9 0.0 copy-start.3
  75.9 1.3 copy-done.3
  77.2 3.3 %copy.39 = bf16[32,8,8,512]{3,2,1,0:T(8,128)(2,1)S(1)} copy(bf16[32,8,8,512]{3,1,0,2:T(8,128)(2,1)} %bitcast.141) | data formatting | bytes 4194304 | tf_op jit(solution)/shard_map/all_to_all | solution.py:106
  80.5 2.8 reshape_reshape.3
  83.3 2.6 reshape.334
  85.9 3.4 %fusion.128 = f32[32,256,16]{1,2,0:T(8,128)S(1)} fusion(bf16[32,256,128]{2,1,0:T(8,128)(2,1)} %reshape_reshape.3, f32[128]{0:T(128)S(1)} %convert_subtract_fusion, f32[32,16]{1,0:T(8,128)S(1)} %copy.40), kind=kOutput, calls=%fused_computation.136 | convolution fusion | flops 201392128 | bytes 2624000 | tf_op jit(solution)/shard_map/dot_general | solution.py:27
  89.2 0.5 reshape.335
  89.7 17.6 %fusion.82 = f32[32,8,32,16]{2,1,3,0:T(8,128)} fusion(f32[32,8,32,16]{2,1,3,0:T(8,128)S(1)} %reshape.335, f32[32,32]{1,0:T(8,128)S(1)} %subtract_maximum_fusion, f32[32,16]{1,0:T(8,128)S(1)} %copy.40, pred[32,32]{1,0:T(8,128)(4,1)S(1)} %broadcast_compare_fusion, f32[32,32,16]{1,2,0:T(8,128)S(1)} %multiply_exponential_fusion), kind=kOutput, calls=%fused_computation.93 | convolution fusion | flops 51511296 | bytes 1121280 | tf_op jit(solution)/shard_map/gkcm,gmcb->gkbm/dot_general | solution.py:50
  107.3 2.1 reshape.336
  109.5 0.0 copy-start.4
  109.5 7.5 %fusion.123 = f32[32,256,128]{2,1,0:T(8,128)S(1)} fusion(f32[32,256,16]{1,2,0:T(8,128)S(1)} %reshape.336, f32[32,16]{1,0:T(8,128)S(1)} %copy.40, f32[32,16]{1,0:T(8,128)S(1)} %copy.44), kind=kOutput, calls=%fused_computation.130 | convolution fusion | flops 201457664 | bytes 4722688 | tf_op jit(solution)/shard_map/dot_general | solution.py:59
  117.0 0.0 copy-done.4
  117.0 9.5 %add_convert_fusion = bf16[32,8,32,128]{3,2,1,0:T(8,128)(2,1)S(1)} fusion(f32[32,8,32,128]{3,2,1,0:T(8,128)S(1)} %bitcast.142, bf16[32,8,32,128]{3,2,1,0:T(8,128)(2,1)S(1)} %copy-done.4, f32[32]{0:T(128)S(1)} %get-tuple-element.29, f32[32]{0:T(128)S(1)} %get-tuple-element.13, f32[32]{0:T(128)S(1)} %get-tuple-element.30, f32[32]{0:T(128)S(1)} %get-tuple-element.14, ...), kind=kOutput, calls=%fused_computation.22 | convolution fusion | flops 1637875712 | bytes 8474624 | tf_op jit(solution)/shard_map/dot_general | solution.py:43
  126.5 6.8 %copy.50 = bf16[32,8,32,128]{0,1,3,2:T(8,128)(2,1)} copy(bf16[32,8,32,128]{3,2,1,0:T(8,128)(2,1)S(1)} %add_convert_fusion) | data formatting | bytes 4194304 | tf_op jit(solution)/shard_map/convert_element_type | solution.py:16
  133.3 10.1 %reshape.351 = bf16[8,2,65536]{2,1,0:T(2,128)(2,1)S(1)} reshape(bf16[4096,8,32]{2,1,0:T(8,128)(2,1)} %bitcast.140) | data formatting | bytes 4194304
  143.5 29.8 %all_to_all.24 = bf16[8,2,65536]{2,1,0:T(2,128)(2,1)} all-to-all(bf16[8,2,65536]{2,1,0:T(2,128)(2,1)S(1)} %reshape.351), channel_id=1, replica_groups=mesh['ctx'=8,'chan'=4] {'ctx'}, dimensions={0} | all-to-all | bytes 4194304 | tf_op jit(solution)/shard_map/all_to_all | solution.py:120
  173.2 8.7 %reshape.352 = bf16[4096,8,32]{2,1,0:T(8,128)(2,1)} reshape(bf16[8,2,65536]{2,1,0:T(2,128)(2,1)} %all_to_all.24) | data formatting | bytes 4194304
  181.9 10.2 %convert_bitcast_fusion = f32[8,32,8,512]{1,2,3,0:T(8,128)} fusion(bf16[32,8,8,512]{0,1,3,2:T(8,128)(2,1)} %bitcast.139), kind=kLoop, calls=%fused_computation | loop fusion | flops 1048576 | bytes 6291456 | tf_op jit(solution)/shard_map/convert_element_type | solution.py:122
  192.1 12.0 %copy.47 = f32[8,32,8,512]{3,2,1,0:T(8,128)} copy(f32[8,32,8,512]{1,2,3,0:T(8,128)} %convert_bitcast_fusion) | data formatting | bytes 8388608 | tf_op jit(solution)/shard_map/convert_element_type | solution.py:122
  204.1 0.0 copy-done.6
  204.1 6.4 %fusion.8 = bf16[2048,512]{1,0:T(8,128)(2,1)S(1)} fusion(f32[3,2048,512]{2,1,0:T(8,128)} %copy-done.2, f32[8,32,8,512]{3,2,1,0:T(8,128)} %copy.47, f32[2048]{0:T(1024)S(1)} %copy-done.6, pred[512]{0:T(512)(128)(4,1)S(1)} %iota_compare_fusion), kind=kLoop, calls=%fused_computation.16 | loop fusion | flops 7340032 | bytes 18883072 | tf_op jit(solution)/shard_map/convert_element_type | solution.py:126
  210.5 14.0 %fusion.5 = bf16[4096,512]{0,1:T(8,128)(2,1)} fusion(bf16[2048,512]{1,0:T(8,128)(2,1)S(1)} %fusion.8, bf16[2048,4096]{1,0:T(8,128)(2,1)} %param.15), kind=kOutput, calls=%fused_computation.11 | convolution fusion | flops 8592031744 | bytes 23068672 | tf_op jit(solution)/shard_map/dot_general | solution.py:128
  224.5 0.0 reduce-scatter.2.cloned.1.call-update
  224.5 0.0 copy-start.1
  224.5 76.3 %reduce-scatter.2.cloned.1.call-done = bf16[1024,512]{0,1:T(8,128)(2,1)} async-done(((bf16[4096,512]{0,1:T(8,128)(2,1)}), bf16[1024,512]{0,1:T(8,128)(2,1)}) %reduce-scatter.2.cloned.1.call-update) | async-done | bytes 1048592 | tf_op jit(solution)/shard_map/reduce_scatter | solution.py:127
  300.8 2.3 copy.48
  303.1 0.0 copy-done.1
  (16 shorter events, 0.1 us)
Async XLA Ops:
  6.5 42.8 %copy-start = (f32[16,256]{1,0:T(8,128)S(1)}, f32[16,256]{1,0:T(8,128)}, u32[]{:S(2)}) copy-start(f32[16,256]{1,0:T(8,128)} %param.13) | copy-start | bytes 49156
  7.2 6.4 %copy-start.8 = (u32[32]{0:T(128)S(1)}, u32[32]{0:T(128)}, u32[]{:S(2)}) copy-start(u32[32]{0:T(128)} %constant.36) | copy-start | bytes 388
  7.2 17.6 %copy-start.5 = (f32[3,3,2048]{2,1,0:T(4,128)S(1)}, f32[3,3,2048]{2,1,0:T(4,128)}, u32[]{:S(2)}) copy-start(f32[3,3,2048]{2,1,0:T(4,128)} %param.9) | copy-start | bytes 221188
  10.6 14.5 %collective-permute-start = (bf16[3,2048,2]{1,0,2:T(4,128)(2,1)S(1)}, bf16[3,2048,2]{1,0,2:T(4,128)(2,1)S(1)}, u32[]{:S(2)}, u32[]{:S(2)}) collective-permute-start(bf16[3,2048,2]{1,0,2:T(4,128)(2,1)S(1)} %copy.54), channel_id=1, source_target_pairs={{0,4},{4,8},{8,12},{12,16},{16,20},{20,24},{24,28},{1,5},{5,9},{9,... | collective-permute-start | bytes 73736 | tf_op jit(solution)/shard_map/ppermute | solution.py:12
  38.5 4.5 %copy-start.2 = (f32[3,2048,512]{2,1,0:T(8,128)}, f32[3,2048,512]{2,1,0:T(8,128)S(1)}, u32[]{:S(2)}) copy-start(f32[3,2048,512]{2,1,0:T(8,128)S(1)} %multiply_add_fusion) | copy-start | bytes 37748740
  45.5 4.1 %copy-start.7 = (f32[16,256]{1,0:T(8,128)S(1)}, f32[16,256]{1,0:T(8,128)}, u32[]{:S(2)}) copy-start(f32[16,256]{1,0:T(8,128)} %param.12) | copy-start | bytes 49156
  45.5 30.3 %all-to-all-start = ((bf16[256,8,512]{2,1,0:T(8,128)(2,1)}), bf16[256,8,512]{2,1,0:T(8,128)(2,1)S(1)}, u32[]{:S(2)}, u32[]{:S(2)}) async-start(bf16[256,8,512]{2,1,0:T(8,128)(2,1)} %fusion.11), calls=%async_computation | async-start | bytes 4194304 | tf_op jit(solution)/shard_map/all_to_all | solution.py:106
  49.3 251.5 %reduce-scatter.2.cloned.1.call-start = ((), (), s32[]{:S(2)}) async-start(), calls=%async_computation.3 | async-start | bytes 5242880 | tf_op jit(solution)/shard_map/reduce_scatter | solution.py:127
  75.9 1.3 copy-start.3
  109.5 7.5 %copy-start.4 = (bf16[32,8,32,128]{3,2,1,0:T(8,128)(2,1)S(1)}, bf16[32,8,32,128]{3,2,1,0:T(8,128)(2,1)}, u32[]{:S(2)}) copy-start(bf16[32,8,32,128]{3,2,1,0:T(8,128)(2,1)} %reshape.334) | copy-start | bytes 6291460
  192.1 12.0 %copy-start.6 = (f32[2048]{0:T(1024)S(1)}, f32[2048]{0:T(1024)}, u32[]{:S(2)}) copy-start(f32[2048]{0:T(1024)} %param.14) | copy-start | bytes 24580
  224.5 78.6 %copy-start.1 = (f32[16,256]{1,0:T(8,128)S(1)}, f32[16,256]{1,0:T(8,128)}, u32[]{:S(2)}) copy-start(f32[16,256]{1,0:T(8,128)} %param.13) | copy-start | bytes 49156
Sparse Core Ops, SparseCore 0:
  224.6 76.1 reduce-scatter.1
where the time goes:
time: 311 us; the launch traced here: 310 us
  waiting for transfers between devices  102 us (33%)
  local copies, waits for them, and re-layouts  63.9 us (21%)
  matrix products  52 us (17%)
  blocking collectives  38.8 us (12%)
  other arithmetic  32.2 us (10%)
  between operations  15 us (5%)
  starting transfers between devices  6.13 us (2%)
    reduce_scatter x1, waiting for transfers between devices, shards(): lax.psum_scatter(lax.dot_general(out_weight, mixed_rows, (((0,), (0,)), (...  76.3 us
    all_to_all x1, blocking collectives, shards(): lax.all_to_all(shortened(result), 'ctx', split_axis=2, concat_axis=0, til...  29.8 us
    unnamed x28, local copies, waits for them, and re-layouts  27.7 us
    all_to_all x1, waiting for transfers between devices, shards(): lax.all_to_all(product.reshape(groups, per_group, slot_count).astype(jnp....  25.6 us
    dot_general x1, matrix products, block_pass(): entering = jnp.einsum('gkcm,gmcb->gkbm', summary, mixing, precision=highest)  17.6 us
    dot_general x1, matrix products, shards(): lax.dot_general(out_weight, mixed_rows, (((0,), (0,)), ((), ())), preferr...  14 us
    add x1, other arithmetic, shards(): short_conv + short_filter[:, tap_index, :, None] * window_rows.astype(jnp...  12.5 us
    convert_element_type x1, local copies, waits for them, and re-layouts, shards(): long_conv = lax.all_to_all(shortened(result), 'ctx', split_axis=2, concat...  12 us
  transfers between devices with their start and end apart: 3, of which 2 were waited for; matrix products, arithmetic and copies ran while one was open for 1% of the time, Pallas kernels for 0%

commit v1 on v0

--- a/solution.py
+++ b/solution.py
@@ -4,6 +4,12 @@
 from jax.sharding import PartitionSpec as P
 
 highest = lax.Precision.HIGHEST
+strings_connect = lambda my_data, which_axis: jnp.concatenate(
+    lax.all_to_all(
+        jnp.stack(jnp.split(my_data, lax.axis_size(which_axis), axis=2), axis=0), which_axis, 0, 0
+    ),
+    axis=0,
+)
 
 
 def passed_along(array, axis, by):
@@ -117,9 +123,7 @@
     )
     outer_part = outer_pass(entering, decay_mine, residue_mine, block_width)
     result = (inner_part + outer_part).reshape(shared, item_count, ctx_count * slot_count)
-    long_conv = lax.all_to_all(
-        shortened(result), "ctx", split_axis=2, concat_axis=0, tiled=True
-    ).astype(result.dtype)
+    long_conv = strings_connect(shortened(result), "ctx").astype(result.dtype)
     long_conv = long_conv.reshape(channels, slot_count)
     mixed_rows = jnp.where(
         usable, short_conv[0] * (long_conv + skip_weight[:, None] * product), 0.0

time: 311 us -> 265 us (0.85)
  local copies, waits for them, and re-layouts: 63.9 us -> 29.3 us
  other arithmetic: 32.2 us -> 15.7 us
  matrix products: 52 us -> 58.4 us
    unnamed x28 -> x33, local copies, waits for them, and re-layouts: 27.7 us -> 9.05 us
    convert_element_type x2 -> x0, other arithmetic: 16.6 us -> none  [the longest x1 10.2 us: shards(): long_conv = lax.all_to_all(shortened(result), 'ctx', split_axis=2, concat...]
    convert_element_type x1 -> x0, local copies, waits for them, and re-layouts: 12 us -> none  [shards(): long_conv = lax.all_to_all(shortened(result), 'ctx', split_axis=2, concat...]
    dot_general x1, matrix products: 14 us -> 20.2 us  [shards(): lax.dot_general(out_weight, mixed_rows, (((0,), (0,)), ((), ())), preferr...]
    convert_element_type x1, local copies, waits for them, and re-layouts: 6.8 us -> 2.82 us  [shortened(): a.astype(jnp.bfloat16)]
where the time goes in v1:
time: 265 us
  waiting for transfers between devices  102 us (38%)
  matrix products  58.4 us (22%)
  blocking collectives  38.1 us (14%)
  local copies, waits for them, and re-layouts  29.3 us (11%)
  other arithmetic  15.7 us (6%)
  between operations  15 us (6%)
  starting transfers between devices  6.13 us (2%)
    reduce_scatter x1, waiting for transfers between devices, shards(): lax.psum_scatter(lax.dot_general(out_weight, mixed_rows, (((0,), (0,)), (...  76.3 us
    all_to_all x1, blocking collectives, lax.all_to_all(jnp.stack(jnp.split(my_data, lax.axis_size(which_axis), ax...  29 us
    all_to_all x1, waiting for transfers between devices, shards(): lax.all_to_all(product.reshape(groups, per_group, slot_count).astype(jnp....  25.6 us
    dot_general x1, matrix products, shards(): lax.dot_general(out_weight, mixed_rows, (((0,), (0,)), ((), ())), preferr...  20.2 us
    dot_general x1, matrix products, block_pass(): entering = jnp.einsum('gkcm,gmcb->gkbm', summary, mixing, precision=highest)  17.7 us
    add x1, other arithmetic, shards(): short_conv + short_filter[:, tap_index, :, None] * window_rows.astype(jnp...  12.6 us
    dot_general x1, matrix products, block_pass(): lax.dot_general(blocks, toeplitz, (((3,), (2,)), ((0,), (0,))), precision...  9.64 us
    unnamed x33, local copies, waits for them, and re-layouts  9.05 us
  transfers between devices with their start and end apart: 3, of which 2 were waited for; matrix products, arithmetic and copies ran while one was open for 1% of the time, Pallas kernels for 0%

profile of v1, /device:TPU:0, one launch (start us, length us, event | category | flops | bytes accessed | tf_op | source)
XLA Modules:
  0.0 264.5 jit_solution(9680521514836836407)
XLA Ops:
  6.5 0.0 copy-start
  7.2 0.0 copy-start.8
  7.2 0.0 copy-start.5
  7.2 2.5 constant_dynamic-slice_fusion
  9.7 0.9 copy.37
  10.6 2.4 collective-permute-start
  13.6 0.0 copy-done.8
  13.6 0.6 dynamic-slice
  14.3 0.7 dynamic-update-slice.1
  15.0 0.7 dynamic-update-slice
  15.8 9.1 %all-reduce.2 = (s32[8]{0:T(128)S(1)}, s32[8]{0:T(128)S(1)}) all-reduce(s32[8]{0:T(128)S(1)} %dynamic-update-slice, s32[8]{0:T(128)S(1)} %dynamic-update-slice.1), channel_id=1, replica_groups=mesh['ctx'=8,'chan'=4] {'ctx'}, use_global_device_ids=true, to_apply=%add | all-reduce | flops 16 | bytes 128
  24.8 0.0 copy-done.5
  24.8 0.1 fusion.167
  24.9 0.1 clamp_convert_fusion
  24.9 0.1 broadcast_add_fusion
  25.1 0.0 collective-permute-done
  25.1 0.9 copy.24
  26.0 12.6 %multiply_add_fusion = f32[3,2048,512]{2,1,0:T(8,128)S(1)} fusion(bf16[3,2048,512]{2,1,0:T(8,128)(2,1)} %param.8, bf16[3,2048,2]{2,1,0:T(8,128)(2,1)S(1)} %copy.24, f32[3,2048]{1,0:T(4,128)S(1)} %get-tuple-element.46, f32[3,2048]{1,0:T(4,128)S(1)} %get-tuple-element.47, f32[3,2048]{1,0:T(4,128)S(1)} %bitcast.168), kind=kLoop, calls=%fused_computation | loop fusion | flops 44040192 | bytes 18972672 | tf_op jit(solution)/shard_map/add | solution.py:94
  38.6 0.0 copy-start.2
  38.6 4.5 %copy-done.2 = f32[3,2048,512]{2,1,0:T(8,128)} copy-done((f32[3,2048,512]{2,1,0:T(8,128)}, f32[3,2048,512]{2,1,0:T(8,128)S(1)}, u32[]{:S(2)}) %copy-start.2) | copy-done | bytes 12582936
  43.1 2.5 fusion.10
  45.6 0.0 copy-start.6
  45.6 3.7 %all-to-all-start = ((bf16[256,8,512]{2,1,0:T(8,128)(2,1)}), bf16[256,8,512]{2,1,0:T(8,128)(2,1)S(1)}, u32[]{:S(2)}, u32[]{:S(2)}) async-start(bf16[256,8,512]{2,1,0:T(8,128)(2,1)} %fusion.10), calls=%async_computation | async-start | bytes 4194304 | tf_op jit(solution)/shard_map/all_to_all | solution.py:112
  49.4 0.0 reduce-scatter.2.cloned.1.call-start
  49.4 0.0 copy-done
  49.4 0.1 dynamic-slice_bitcast_fusion.1
  49.5 0.1 convert_element_type.133
  49.6 0.1 add.115
  49.7 0.1 copy.30
  49.8 0.0 copy-done.6
  49.8 0.1 fusion.166
  49.8 0.1 copy.26
  49.9 0.1 copy.29
  50.1 0.1 broadcast_compare_fusion
  50.2 0.1 subtract_maximum_fusion
  50.3 0.1 multiply_exponential_fusion
  50.4 25.6 %all-to-all-done = bf16[256,8,512]{2,1,0:T(8,128)(2,1)S(1)} async-done(((bf16[256,8,512]{2,1,0:T(8,128)(2,1)}), bf16[256,8,512]{2,1,0:T(8,128)(2,1)S(1)}, u32[]{:S(2)}, u32[]{:S(2)}) %all-to-all-start) | async-done | bytes 2097184 | tf_op jit(solution)/shard_map/all_to_all | solution.py:112
  76.0 0.0 copy-start.3
  76.0 1.3 copy-done.3
  77.3 3.3 %copy.25 = bf16[32,8,8,512]{3,2,1,0:T(8,128)(2,1)S(1)} copy(bf16[32,8,8,512]{3,1,0,2:T(8,128)(2,1)} %bitcast.165) | data formatting | bytes 4194304 | tf_op jit(solution)/shard_map/all_to_all | solution.py:112
  80.6 2.8 %reshape_reshape.3 = bf16[32,256,128]{2,1,0:T(8,128)(2,1)} reshape(bf16[32,8,8,512]{3,2,1,0:T(8,128)(2,1)S(1)} %copy.25) | data formatting | bytes 4194304 | tf_op jit(solution)/shard_map/reshape;reshape | solution.py:34
  83.4 2.6 reshape.333
  86.0 3.4 %fusion.139 = f32[32,256,16]{1,2,0:T(8,128)S(1)} fusion(bf16[32,256,128]{2,1,0:T(8,128)(2,1)} %reshape_reshape.3, f32[128]{0:T(128)S(1)} %convert_subtract_fusion, f32[32,16]{1,0:T(8,128)S(1)} %copy.26), kind=kOutput, calls=%fused_computation.154 | convolution fusion | flops 201392128 | bytes 2624000 | tf_op jit(solution)/shard_map/dot_general | solution.py:33
  89.4 0.5 reshape.334
  89.9 17.7 %fusion.85 = f32[32,8,32,16]{2,1,3,0:T(8,128)} fusion(f32[32,8,32,16]{2,1,3,0:T(8,128)S(1)} %reshape.334, f32[32,32]{1,0:T(8,128)S(1)} %subtract_maximum_fusion, f32[32,16]{1,0:T(8,128)S(1)} %copy.26, pred[32,32]{1,0:T(8,128)(4,1)S(1)} %broadcast_compare_fusion, f32[32,32,16]{1,2,0:T(8,128)S(1)} %multiply_exponential_fusion), kind=kOutput, calls=%fused_computation.95 | convolution fusion | flops 51511296 | bytes 1121280 | tf_op jit(solution)/shard_map/gkcm,gmcb->gkbm/dot_general | solution.py:56
  107.5 2.1 reshape.335
  109.6 0.0 copy-start.4
  109.7 7.5 %fusion.134 = f32[32,256,128]{2,1,0:T(8,128)S(1)} fusion(f32[32,256,16]{1,2,0:T(8,128)S(1)} %reshape.335, f32[32,16]{1,0:T(8,128)S(1)} %copy.26, f32[32,16]{1,0:T(8,128)S(1)} %copy.30), kind=kOutput, calls=%fused_computation.148 | convolution fusion | flops 201457664 | bytes 4722688 | tf_op jit(solution)/shard_map/dot_general | solution.py:65
  117.2 0.0 copy-done.4
  117.2 9.6 %add_convert_fusion = bf16[32,8,32,128]{3,2,1,0:T(8,128)(2,1)} fusion(f32[32,8,32,128]{3,2,1,0:T(8,128)S(1)} %bitcast.166, bf16[32,8,32,128]{3,2,1,0:T(8,128)(2,1)S(1)} %copy-done.4, f32[32]{0:T(128)S(1)} %get-tuple-element.29, f32[32]{0:T(128)S(1)} %get-tuple-element.13, f32[32]{0:T(128)S(1)} %get-tuple-element.30, f32[32]{0:T(128)S(1)} %get-tuple-element.14, ...), kind=kOutput, calls=%fused_computation.21 | convolution fusion | flops 1637875712 | bytes 8474624 | tf_op jit(solution)/shard_map/dot_general | solution.py:49
  126.8 2.8 %convert_element_type.136 = bf16[32,8,4096]{2,1,0:T(8,128)(2,1)S(1)} reshape(bf16[32,8,32,128]{3,2,1,0:T(8,128)(2,1)} %add_convert_fusion) | data formatting | bytes 4194304 | tf_op jit(solution)/shard_map/convert_element_type | solution.py:22
  129.9 0.0 copy-start.7
  129.9 29.0 %all_to_all.20 = bf16[8,32,8,512]{3,2,1,0:T(8,128)(2,1)S(1)} all-to-all(bf16[8,32,8,512]{3,2,1,0:T(8,128)(2,1)S(1)} %fusion.126), channel_id=1, replica_groups=mesh['ctx'=8,'chan'=4] {'ctx'}, dimensions={0} | all-to-all | bytes 4194304 | tf_op jit(solution)/shard_map/all_to_all | solution.py:8
  158.9 0.0 copy-done.7
  158.9 20.2 %fusion.5 = bf16[4096,512]{0,1:T(8,128)(2,1)} fusion(bf16[2048,4096]{1,0:T(8,128)(2,1)} %param.15, f32[3,2048,512]{2,1,0:T(8,128)} %copy-done.2, bf16[2048,512]{1,0:T(8,128)(2,1)S(1)} %bitcast.167, f32[2048]{0:T(1024)S(1)} %copy-done.7, pred[512]{0:T(512)(128)(4,1)S(1)} %iota_compare_fusion), kind=kOutput, calls=%fused_computation.10 | convolution fusion | flops 8600420352 | bytes 35660288 | tf_op jit(solution)/shard_map/dot_general | solution.py:132
  179.1 0.0 reduce-scatter.2.cloned.1.call-update
  179.1 0.0 copy-start.1
  179.2 76.3 %reduce-scatter.2.cloned.1.call-done = bf16[1024,512]{0,1:T(8,128)(2,1)} async-done(((bf16[4096,512]{0,1:T(8,128)(2,1)}), bf16[1024,512]{0,1:T(8,128)(2,1)}) %reduce-scatter.2.cloned.1.call-update) | async-done | bytes 1048592 | tf_op jit(solution)/shard_map/reduce_scatter | solution.py:131
  255.4 2.3 copy.32
  257.7 0.0 copy-done.1
  (23 shorter events, 0.3 us)
Async XLA Ops:
  6.5 42.9 %copy-start = (f32[16,256]{1,0:T(8,128)S(1)}, f32[16,256]{1,0:T(8,128)}, u32[]{:S(2)}) copy-start(f32[16,256]{1,0:T(8,128)} %param.13) | copy-start | bytes 49156
  7.2 6.4 %copy-start.8 = (u32[32]{0:T(128)S(1)}, u32[32]{0:T(128)}, u32[]{:S(2)}) copy-start(u32[32]{0:T(128)} %constant.36) | copy-start | bytes 388
  7.2 17.6 %copy-start.5 = (f32[3,3,2048]{2,1,0:T(4,128)S(1)}, f32[3,3,2048]{2,1,0:T(4,128)}, u32[]{:S(2)}) copy-start(f32[3,3,2048]{2,1,0:T(4,128)} %param.9) | copy-start | bytes 221188
  10.6 14.5 %collective-permute-start = (bf16[3,2048,2]{1,0,2:T(4,128)(2,1)S(1)}, bf16[3,2048,2]{1,0,2:T(4,128)(2,1)S(1)}, u32[]{:S(2)}, u32[]{:S(2)}) collective-permute-start(bf16[3,2048,2]{1,0,2:T(4,128)(2,1)S(1)} %copy.37), channel_id=1, source_target_pairs={{0,4},{4,8},{8,12},{12,16},{16,20},{20,24},{24,28},{1,5},{5,9},{9,... | collective-permute-start | bytes 73736 | tf_op jit(solution)/shard_map/ppermute | solution.py:18
  38.6 4.5 %copy-start.2 = (f32[3,2048,512]{2,1,0:T(8,128)}, f32[3,2048,512]{2,1,0:T(8,128)S(1)}, u32[]{:S(2)}) copy-start(f32[3,2048,512]{2,1,0:T(8,128)S(1)} %multiply_add_fusion) | copy-start | bytes 37748740
  45.6 4.1 %copy-start.6 = (f32[16,256]{1,0:T(8,128)S(1)}, f32[16,256]{1,0:T(8,128)}, u32[]{:S(2)}) copy-start(f32[16,256]{1,0:T(8,128)} %param.12) | copy-start | bytes 49156
  45.6 30.3 %all-to-all-start = ((bf16[256,8,512]{2,1,0:T(8,128)(2,1)}), bf16[256,8,512]{2,1,0:T(8,128)(2,1)S(1)}, u32[]{:S(2)}, u32[]{:S(2)}) async-start(bf16[256,8,512]{2,1,0:T(8,128)(2,1)} %fusion.10), calls=%async_computation | async-start | bytes 4194304 | tf_op jit(solution)/shard_map/all_to_all | solution.py:112
  49.4 206.0 %reduce-scatter.2.cloned.1.call-start = ((), (), s32[]{:S(2)}) async-start(), calls=%async_computation.3 | async-start | bytes 5242880 | tf_op jit(solution)/shard_map/reduce_scatter | solution.py:131
  76.0 1.3 copy-start.3
  109.6 7.5 %copy-start.4 = (bf16[32,8,32,128]{3,2,1,0:T(8,128)(2,1)S(1)}, bf16[32,8,32,128]{3,2,1,0:T(8,128)(2,1)}, u32[]{:S(2)}) copy-start(bf16[32,8,32,128]{3,2,1,0:T(8,128)(2,1)} %reshape.333) | copy-start | bytes 6291460
  129.9 29.1 %copy-start.7 = (f32[2048]{0:T(1024)S(1)}, f32[2048]{0:T(1024)}, u32[]{:S(2)}) copy-start(f32[2048]{0:T(1024)} %param.14) | copy-start | bytes 24580
  179.1 78.6 %copy-start.1 = (f32[16,256]{1,0:T(8,128)S(1)}, f32[16,256]{1,0:T(8,128)}, u32[]{:S(2)}) copy-start(f32[16,256]{1,0:T(8,128)} %param.13) | copy-start | bytes 49156
Sparse Core Ops, SparseCore 0:
  179.3 76.1 reduce-scatter.1
